TPU v7x, 32 devices: a whole 2x2x4 slice. The times are simulated.
32 devices in a mesh: shot: 8 (over y, x, core), rcv: 4 (over z).
Axes of the slice: x: 2, y: 2, z: 4, core: 2. Of those that a mesh axis runs over, the one named last changes fastest.
Arguments:
- spectra: bfloat16 [4, 2, 2048, 2048], P(None, None, 'shot', 'rcv'), may hold values from -6 to 6
Outputs:
- multiples: float32 [4, 2, 2048, 2048], P('rcv', None, 'shot')
All inputs are finite; a program needn't handle non-finite values.
Results may differ from a plain program's by a relative error of at most 0.0003.
Values may be sent and summed in bfloat16 or wider, within the bound.
A program may use at most 128 MiB of HBM per device.

v0:
```python
import math

import jax
import jax.numpy as jnp
from jax import lax
from jax.sharding import PartitionSpec as P


def per_device(spectra):
    own_rows = lax.all_to_all(spectra, "rcv", split_axis=0, concat_axis=3, tiled=True)
    receiver_set_full = own_rows.shape[3]
    real_left_gathered = own_rows[:, 0]
    imaginary_left_gathered = own_rows[:, 1]
    shard_part = lax.all_gather(own_rows, "shot", axis=2, tiled=True)
    real_right_factor = shard_part[:, 0]
    imaginary_right_factor = shard_part[:, 1]
    real_out = jnp.einsum(
        "ang,agv->anv", real_left_gathered, real_right_factor, preferred_element_type=jnp.float32
    ) - jnp.einsum(
        "ang,agv->anv",
        imaginary_left_gathered,
        imaginary_right_factor,
        preferred_element_type=jnp.float32,
    )
    imag_out = jnp.einsum(
        "ang,agv->anv",
        real_left_gathered,
        imaginary_right_factor,
        preferred_element_type=jnp.float32,
    ) + jnp.einsum(
        "ang,agv->anv",
        imaginary_left_gathered,
        real_right_factor,
        preferred_element_type=jnp.float32,
    )
    result = jnp.stack([real_out, imag_out], axis=1)
    return result * (-1.0 / math.sqrt(receiver_set_full))


def solution(mesh):
    return jax.shard_map(
        per_device,
        mesh=mesh,
        in_specs=(P(None, None, "shot", "rcv"),),
        out_specs=P("rcv", None, "shot", None),
        check_vma=False,
    )
```

profile of v0, /device:TPU:1, one launch (start us, length us, event | category | flops | bytes accessed | tf_op | source)
XLA Modules:
  0.0 186.3 jit_solution(3624461053671120266)
XLA Ops:
  6.5 0.0 all-gather.2.cloned.1.call-start
  6.5 2.8 %copy.3 = bf16[4,2,256,512]{2,3,1,0:T(8,128)(2,1)S(1)} copy(bf16[4,2,256,512]{3,2,1,0:T(8,128)(2,1)} %param.1) | data formatting | bytes 4194304 | tf_op args[0]
  9.3 52.6 %all_to_all.18 = bf16[4,2,256,512]{2,3,1,0:T(8,128)(2,1)S(1)} all-to-all(bf16[4,2,256,512]{2,3,1,0:T(8,128)(2,1)S(1)} %copy.3), channel_id=1, replica_groups=mesh['shot'=8,'rcv'=4] {'rcv'}, dimensions={0} | all-to-all | bytes 4194304 | tf_op jit(solution)/shard_map/all_to_all | solution.py:10
  61.9 1.5 copy.4
  63.3 0.0 copy-start
  63.3 0.0 all-gather.2.cloned.1.call-update
  63.3 94.1 %all-gather.2.cloned.1.call-done = bf16[1,2,2048,2048]{2,3,1,0:T(8,128)(2,1)} async-done(((bf16[1,2,256,2048]{2,3,1,0:T(8,128)(2,1)}), bf16[1,2,2048,2048]{2,3,1,0:T(8,128)(2,1)}) %all-gather.2.cloned.1.call-update) | async-done | bytes 16777232 | tf_op jit(solution)/shard_map/all_gather | solution.py:14
  157.4 0.0 copy-done
  157.4 0.0 slice-start
  157.4 0.0 slice-start.1
  157.4 0.0 slice-start.2
  157.4 5.9 %fusion = f32[256,2048]{1,0:T(8,128)S(1)} fusion(bf16[1,2,2048,2048]{2,3,1,0:T(8,128)(2,1)} %all-gather.2.cloned.1.call-done, bf16[1,2,256,2048]{2,3,1,0:T(8,128)(2,1)S(1)} %bitcast.34), kind=kOutput, calls=%fused_computation.2 | convolution fusion | flops 2147483648 | bytes 11534336 | tf_op jit(solution)/shard_map/ang,agv->anv/dot_general | solution.py:30
  163.3 0.0 slice-start.3
  163.3 7.2 %fusion.1 = f32[256,2048]{1,0:T(8,128)} fusion(bf16[1,2,2048,2048]{2,3,1,0:T(8,128)(2,1)} %all-gather.2.cloned.1.call-done, bf16[1,2,256,2048]{2,3,1,0:T(8,128)(2,1)S(1)} %bitcast.35), kind=kOutput, calls=%fused_computation.3 | convolution fusion | flops 2147483648 | bytes 11534336 | tf_op jit(solution)/shard_map/ang,agv->anv/dot_general | solution.py:17
  170.6 0.0 slice-done
  170.6 0.0 slice-done.1
  170.6 0.0 slice-done.2
  170.6 0.0 slice-done.3
  170.6 2.4 %fusion.7 = f32[1,1,256,2048]{3,2,1,0:T(8,128)S(1)} fusion(f32[256,2048]{1,0:T(8,128)S(1)} %fusion, bf16[1,2,2048,2048]{2,3,1,0:T(8,128)(2,1)S(1)} %bitcast.39, bf16[1,2,256,2048]{2,3,1,0:T(8,128)(2,1)S(1)} %bitcast.36), kind=kOutput, calls=%fused_computation.10 | convolution fusion | flops 2148007936 | bytes 13631488 | tf_op jit(solution)/shard_map/ang,agv->anv/dot_general | solution.py:25
  173.0 4.0 %fusion.5 = f32[1,1,256,2048]{3,2,1,0:T(8,128)S(1)} fusion(f32[256,2048]{1,0:T(8,128)} %fusion.1, bf16[1,2,2048,2048]{2,3,1,0:T(8,128)(2,1)S(1)} %bitcast.39, bf16[1,2,256,2048]{2,3,1,0:T(8,128)(2,1)S(1)} %bitcast.37), kind=kOutput, calls=%fused_computation.8 | convolution fusion | flops 2148007936 | bytes 13631488 | tf_op jit(solution)/shard_map/ang,agv->anv/dot_general | solution.py:19
  177.0 2.4 %maximum_multiply_fusion = f32[1,2,256,2048]{3,2,1,0:T(8,128)} fusion(f32[1,1,256,2048]{3,2,1,0:T(8,128)S(1)} %fusion.7, f32[1,1,256,2048]{3,2,1,0:T(8,128)S(1)} %fusion.5), kind=kLoop, calls=%fused_computation.6 | loop fusion | flops 2097152 | bytes 8388608 | tf_op jit(solution)/shard_map/mul | solution.py:37
  (1 shorter events, 0.0 us)
Async XLA Ops:
  6.5 150.9 %all-gather.2.cloned.1.call-start = ((), (), s32[]{:S(2)}) async-start(), calls=%async_computation.1 | async-start | bytes 18874368 | tf_op jit(solution)/shard_map/all_gather | solution.py:14
  63.3 94.1 %copy-start = (bf16[4,2,256,512]{2,3,0,1:T(8,128)(2,1)S(1)}, bf16[4,2,256,512]{2,3,0,1:T(8,128)(2,1)}, u32[]{:S(2)}) copy-start(bf16[4,2,256,512]{2,3,0,1:T(8,128)(2,1)} %copy.4) | copy-start | bytes 6291460
  157.4 13.2 %slice-start = ((s8[16777216]{0:T(1024)(128)(4,1)}), s8[4194304]{0:T(1024)(128)(4,1)S(1)}, s32[]{:S(2)}) async-start(s8[16777216]{0:T(1024)(128)(4,1)} %bitcast.38), calls=%async_computation.2 | async-start | bytes 8388608
  157.4 13.2 %slice-start.1 = ((s8[16777216]{0:T(1024)(128)(4,1)}), s8[4194304]{0:T(1024)(128)(4,1)S(1)}, s32[]{:S(2)}) async-start(s8[16777216]{0:T(1024)(128)(4,1)} %bitcast.38), calls=%async_computation.3 | async-start | bytes 8388608
  157.4 13.2 %slice-start.2 = ((s8[16777216]{0:T(1024)(128)(4,1)}), s8[4194304]{0:T(1024)(128)(4,1)S(1)}, s32[]{:S(2)}) async-start(s8[16777216]{0:T(1024)(128)(4,1)} %bitcast.38), calls=%async_computation.4 | async-start | bytes 8388608
  163.3 7.3 %slice-start.3 = ((s8[16777216]{0:T(1024)(128)(4,1)}), s8[4194304]{0:T(1024)(128)(4,1)S(1)}, s32[]{:S(2)}) async-start(s8[16777216]{0:T(1024)(128)(4,1)} %bitcast.38), calls=%async_computation.5 | async-start | bytes 8388608
Sparse Core Ops, SparseCore 0:
  63.5 93.8 all-gather.1
where the time goes:
time: 187 us; the launch traced here: 186 us
  waiting for transfers between devices  94.1 us (50%)
  blocking collectives  52.6 us (28%)
  matrix products  19.5 us (10%)
  between operations  13.5 us (7%)
  local copies, waits for them, and re-layouts  4.23 us (2%)
  other arithmetic  2.43 us (1%)
    all_gather x1, waiting for transfers between devices, per_device(): shard_part = lax.all_gather(own_rows, 'shot', axis=2, tiled=True)  94.1 us
    all_to_all x1, blocking collectives, per_device(): lax.all_to_all(spectra, 'rcv', split_axis=0, concat_axis=3, tiled=True)  52.6 us
    dot_general x1, matrix products, per_device(): jnp.einsum('ang,agv->anv', real_left_gathered, real_right_factor, preferr...  7.24 us
    dot_general x1, matrix products, per_device(): jnp.einsum('ang,agv->anv', imaginary_left_gathered, real_right_factor, pr...  5.91 us
    dot_general x1, matrix products, per_device(): jnp.einsum('ang,agv->anv', imaginary_left_gathered, imaginary_right_facto...  3.98 us
  transfers between devices with their start and end apart: 1, of which 1 were waited for; matrix products, arithmetic and copies ran while one was open for 0% of the time, Pallas kernels for 0%

commit v1 on v0

v1 whole, which is shorter than its diff:
```python
import functools
import math

import jax
import jax.numpy as jnp
from jax import lax
from jax.experimental import pallas as pl
from jax.experimental.pallas import tpu as pltpu
from jax.sharding import PartitionSpec as P

MESH = pl.DeviceIdType.MESH
PLANE = 8
LINE = 4

FROM_X, FROM_Y, DIAGONAL = 0, 2, 4
CORE_OWN, CORE_X, CORE_Y, CORE_DIAGONAL = 6, 8, 10, 12
KINDS = 14


def kernel(rows, cols, scale, x_ref, out_ref, g, own_sem, line_send, line_recv, send, recv):
    s, z = lax.axis_index("shot"), lax.axis_index("rcv")
    y, x, c = s // 4, (s // 2) % 2, s % 2
    sx = y * 4 + (1 - x) * 2 + c
    sy = (1 - y) * 4 + x * 2 + c
    sd = (1 - y) * 4 + (1 - x) * 2 + c
    sc = y * 4 + x * 2 + (1 - c)
    half = z // 2
    u = z + half * (3 - 2 * z)

    def mirrored(v):
        return v + half * (3 - 2 * v)

    order = [z, mirrored(1 - u), mirrored(2), mirrored(3)]
    others = order[1:]

    barrier = pltpu.get_barrier_semaphore()
    for peer in (sx, sy, sc):
        pl.semaphore_signal(barrier, inc=1, device_id=(peer, z), device_id_type=MESH)
    for peer in others:
        pl.semaphore_signal(barrier, inc=1, device_id=(s, peer), device_id_type=MESH)
    pl.semaphore_wait(barrier, 6)

    def block(column, part, shot):
        return g.at[part, column, pl.ds(shot * rows, rows), :]

    def along_line(peer, part):
        return pltpu.make_async_remote_copy(
            src_ref=x_ref.at[peer, part],
            dst_ref=block(z, part, s),
            send_sem=line_send.at[peer, part],
            recv_sem=line_recv.at[z, part],
            device_id=(s, peer),
            device_id_type=MESH,
        )

    def line_arrival(source, part):
        return pltpu.make_async_remote_copy(
            src_ref=x_ref.at[source, part],
            dst_ref=block(source, part, s),
            send_sem=line_send.at[source, part],
            recv_sem=line_recv.at[source, part],
            device_id=(s, source),
            device_id_type=MESH,
        )

    started = []

    def push(rnd, kind, part, shot, target, source=None):
        place = block(order[rnd], part, shot)
        copy = pltpu.make_async_remote_copy(
            src_ref=place if source is None else source,
            dst_ref=place,
            send_sem=send.at[rnd, kind + part],
            recv_sem=recv.at[rnd, kind + part],
            device_id=(target, z),
            device_id_type=MESH,
        )
        copy.start()
        started.append(copy)

    def arrive(rnd, kind, part, shot):
        place = block(order[rnd], part, shot)
        pltpu.make_async_remote_copy(
            src_ref=place,
            dst_ref=place,
            send_sem=send.at[rnd, kind + part],
            recv_sem=recv.at[rnd, kind + part],
            device_id=(sx, z),
            device_id_type=MESH,
        ).wait_recv()

    def send_own(rnd):
        for part, kind, target in ((0, FROM_X, sx), (1, FROM_Y, sy), (1, FROM_X, sx), (0, FROM_Y, sy)):
            push(rnd, kind, part, s, target, x_ref.at[z, part] if rnd == 0 else None)
        for part in range(2):
            push(rnd, CORE_OWN, part, s, sc, x_ref.at[z, part] if rnd == 0 else None)

    def relay(rnd):
        arrive(rnd, FROM_X, 0, sx)
        push(rnd, DIAGONAL, 0, sx, sy)
        arrive(rnd, FROM_Y, 1, sy)
        push(rnd, DIAGONAL, 1, sy, sx)
        push(rnd, CORE_X, 0, sx, sc)
        push(rnd, CORE_Y, 1, sy, sc)

    def finish_direct(rnd):
        arrive(rnd, FROM_X, 1, sx)
        push(rnd, CORE_X, 1, sx, sc)
        arrive(rnd, FROM_Y, 0, sy)
        push(rnd, CORE_Y, 0, sy, sc)

    def finish_diagonal(rnd):
        for part in range(2):
            arrive(rnd, DIAGONAL, part, sd)
            push(rnd, CORE_DIAGONAL, part, sd, sc)

    def from_core(rnd, kind, shot):
        for part in range(2):
            arrive(rnd, kind, part, shot)

    def twin(shot):
        return shot + 1 - 2 * c

    def drain(rnd):
        from_core(rnd, CORE_OWN, sc)
        from_core(rnd, CORE_X, twin(sx))
        from_core(rnd, CORE_Y, twin(sy))
        from_core(rnd, CORE_DIAGONAL, twin(sd))

    tile = 256

    def chip_product(column, chip, lanes):
        left = [g[part, chip, pl.ds(s * rows, rows), :] for part in range(2)]
        deep = pl.ds(chip * cols, cols)
        right = [g[part, column, deep, lanes] for part in range(2)]
        dot = functools.partial(jnp.dot, preferred_element_type=jnp.float32)
        real = dot(left[0], right[0]) - dot(left[1], right[1])
        imag = dot(left[0], right[1]) + dot(left[1], right[0])
        return real, imag

    def multiply(rnd, chips, first, last):
        column = order[rnd]

        @pl.loop(0, cols // tile)
        def _(t):
            lanes = pl.ds(pl.multiple_of(t * tile, tile), tile)
            wide = pl.ds(pl.multiple_of(column * cols + t * tile, tile), tile)
            real = imag = None
            for chip in chips:
                a, b = chip_product(column, chip, lanes)
                real = a if real is None else real + a
                imag = b if imag is None else imag + b
            if not first:
                real = real + out_ref[0, 0, :, wide]
                imag = imag + out_ref[0, 1, :, wide]
            out_ref[0, 0, :, wide] = real * scale if last else real
            out_ref[0, 1, :, wide] = imag * scale if last else imag

    every = range(LINE)

    own = pltpu.make_async_copy(x_ref.at[z], g.at[:, z, pl.ds(s * rows, rows), :], own_sem)
    own.start()
    line = [along_line(peer, part) for peer in others for part in range(2)]

    def line_step(i):
        for part in range(2):
            line[2 * i + part].start()

    def line_sent(i):
        for part in range(2):
            line[2 * i + part].wait_send()

    line_step(0)
    send_own(0)
    own.wait()
    relay(0)
    line_sent(0)
    line_step(1)
    for rnd in range(1, LINE):
        for part in range(2):
            line_arrival(order[rnd], part).wait_recv()
        send_own(rnd)
        if rnd < LINE - 1:
            line_sent(rnd)
            if rnd + 1 < LINE - 1:
                line_step(rnd + 1)
        finish_direct(rnd - 1)
        finish_diagonal(rnd - 1)
        if rnd == LINE - 1:
            for done in range(LINE - 2):
                drain(done)
                multiply(done, every, True, True)
        relay(rnd)
    last = LINE - 1
    drain(last - 1)
    multiply(last - 1, every, True, True)
    finish_direct(last)
    from_core(last, CORE_OWN, sc)
    multiply(last, [s // 2], True, False)
    from_core(last, CORE_X, twin(sx))
    multiply(last, [sx // 2], False, False)
    from_core(last, CORE_Y, twin(sy))
    multiply(last, [sy // 2], False, False)
    finish_diagonal(last)
    from_core(last, CORE_DIAGONAL, twin(sd))
    multiply(last, [sd // 2], False, True)
    for copy in started:
        copy.wait_send()


def in_one_kernel(spectra):
    freqs, parts, rows, cols = spectra.shape
    full = cols * LINE
    return pl.pallas_call(
        functools.partial(kernel, rows, cols, -1.0 / math.sqrt(full)),
        out_shape=jax.ShapeDtypeStruct((1, parts, rows, full), jnp.float32),
        in_specs=[pl.BlockSpec(memory_space=pl.ANY)],
        out_specs=pl.BlockSpec(memory_space=pltpu.VMEM),
        scratch_shapes=[
            pltpu.VMEM((parts, LINE, rows * PLANE, cols), jnp.bfloat16),
            pltpu.SemaphoreType.DMA,
            pltpu.SemaphoreType.DMA((LINE, 2)),
            pltpu.SemaphoreType.DMA((LINE, 2)),
            pltpu.SemaphoreType.DMA((LINE, KINDS)),
            pltpu.SemaphoreType.DMA((LINE, KINDS)),
        ],
        compiler_params=pltpu.CompilerParams(
            collective_id=0, has_side_effects=True, vmem_limit_bytes=62 * 2**20
        ),
    )(spectra)


def by_collectives(spectra):
    own_rows = lax.all_to_all(spectra, "rcv", split_axis=0, concat_axis=3, tiled=True)
    full = own_rows.shape[3]
    gathered = lax.all_gather(own_rows, "shot", axis=2, tiled=True)
    dot = functools.partial(jnp.einsum, "ang,agv->anv", preferred_element_type=jnp.float32)
    real = dot(own_rows[:, 0], gathered[:, 0]) - dot(own_rows[:, 1], gathered[:, 1])
    imag = dot(own_rows[:, 0], gathered[:, 1]) + dot(own_rows[:, 1], gathered[:, 0])
    return jnp.stack([real, imag], axis=1) * (-1.0 / math.sqrt(full))


def solution(mesh):
    fits = mesh.shape["shot"] == PLANE and mesh.shape["rcv"] == LINE
    return jax.shard_map(
        in_one_kernel if fits else by_collectives,
        mesh=mesh,
        in_specs=(P(None, None, "shot", "rcv"),),
        out_specs=P("rcv", None, "shot", None),
        check_vma=False,
    )
```

time: 187 us -> 107 us (0.57)
  Pallas kernels: 0 us -> 102 us
  waiting for transfers between devices: 94.1 us -> 0 us
  blocking collectives: 52.6 us -> 0 us
  matrix products: 19.5 us -> 0 us
  between operations: 13.5 us -> 0.01 us
  other arithmetic: 2.43 us -> 0 us
    pallas_call x0 -> x1, Pallas kernels: none -> 102 us  [in_one_kernel(): pl.pallas_call(functools.partial(kernel, rows, cols, -1.0 / math.sqrt(ful...]
    all_gather x1 -> x0, waiting for transfers between devices: 94.1 us -> none  [per_device(): shard_part = lax.all_gather(own_rows, 'shot', axis=2, tiled=True)]
    all_to_all x1 -> x0, blocking collectives: 52.6 us -> none  [per_device(): lax.all_to_all(spectra, 'rcv', split_axis=0, concat_axis=3, tiled=True)]
    dot_general x4 -> x0, matrix products: 19.5 us -> none  [the longest x1 7.24 us: per_device(): jnp.einsum('ang,agv->anv', real_left_gathered, real_right_factor, preferr...]
    mul x1 -> x0, other arithmetic: 2.43 us -> none  [per_device(): return result * (-1.0 / math.sqrt(receiver_set_full))]
    unnamed x11 -> x1, local copies, waits for them, and re-layouts: 2.78 us -> 4.7 us
  transfers between devices with their start and end apart: 1 -> 0, of which waited for: 1 -> 0; matrix products, arithmetic and copies ran while one was open for 0% -> 0% of each run, Pallas kernels for 0% -> 0%
where the time goes in v1:
time: 107 us; the launch traced here: 106 us
  Pallas kernels  102 us (95%)
  local copies, waits for them, and re-layouts  4.7 us (4%)
    pallas_call x1, Pallas kernels, in_one_kernel(): pl.pallas_call(functools.partial(kernel, rows, cols, -1.0 / math.sqrt(ful...  102 us
    unnamed x1, local copies, waits for them, and re-layouts  4.7 us

profile of v1, /device:TPU:1, one launch (start us, length us, event | category | flops | bytes accessed | tf_op | source)
XLA Modules:
  0.0 106.5 jit_solution(7619164912721562086)
XLA Ops:
  0.0 101.8 %shard_map.17 = f32[1,2,256,2048]{3,2,1,0:T(8,128)} custom-call(bf16[4,2,256,512]{3,2,1,0:T(8,128)(2,1)} %x_ref.1), custom_call_target="tpu_custom_call" | custom-call | tf_op jit(solution)/shard_map/pallas_call | solution.py:214
  101.8 4.7 %copy.3 = f32[1,2,256,2048]{3,2,1,0:T(8,128)} copy(f32[1,2,256,2048]{3,2,1,0:T(8,128)} %shard_map.17) | data formatting | bytes 8388608

commit v2 on v1

--- a/solution.py
+++ b/solution.py
@@ -17,7 +17,7 @@
 KINDS = 14
 
 
-def kernel(rows, cols, scale, x_ref, out_ref, g, own_sem, line_send, line_recv, send, recv):
+def kernel(rows, cols, scale, x_ref, out_ref, g, acc, own_sem, out_sem, line_send, line_recv, send, recv):
     s, z = lax.axis_index("shot"), lax.axis_index("rcv")
     y, x, c = s // 4, (s // 2) % 2, s % 2
     sx = y * 4 + (1 - x) * 2 + c
@@ -151,49 +151,61 @@
                 real = a if real is None else real + a
                 imag = b if imag is None else imag + b
             if not first:
-                real = real + out_ref[0, 0, :, wide]
-                imag = imag + out_ref[0, 1, :, wide]
-            out_ref[0, 0, :, wide] = real * scale if last else real
-            out_ref[0, 1, :, wide] = imag * scale if last else imag
+                real = real + acc[0, :, wide]
+                imag = imag + acc[1, :, wide]
+            acc[0, :, wide] = real * scale if last else real
+            acc[1, :, wide] = imag * scale if last else imag
+
+    def deliver(rnd):
+        lanes = pl.ds(pl.multiple_of(order[rnd] * cols, cols), cols)
+        return pltpu.make_async_copy(acc.at[:, :, lanes], out_ref.at[0, :, :, lanes], out_sem.at[rnd])
 
     every = range(LINE)
 
     own = pltpu.make_async_copy(x_ref.at[z], g.at[:, z, pl.ds(s * rows, rows), :], own_sem)
     own.start()
-    line = [along_line(peer, part) for peer in others for part in range(2)]
-
-    def line_step(i):
-        for part in range(2):
-            line[2 * i + part].start()
-
-    def line_sent(i):
-        for part in range(2):
-            line[2 * i + part].wait_send()
-
-    line_step(0)
+    def toward(peer, begin):
+        for part in range(2):
+            copy = along_line(peer, part)
+            copy.start() if begin else copy.wait_send()
+
+    toward(others[0], True)
     send_own(0)
+
+    @pl.when(u == 1)
+    def _():
+        toward(others[1], True)
+
     own.wait()
     relay(0)
-    line_sent(0)
-    line_step(1)
+
+    @pl.when(u == 1)
+    def _():
+        toward(others[1], False)
+        toward(others[2], True)
+
     for rnd in range(1, LINE):
         for part in range(2):
             line_arrival(order[rnd], part).wait_recv()
         send_own(rnd)
-        if rnd < LINE - 1:
-            line_sent(rnd)
-            if rnd + 1 < LINE - 1:
-                line_step(rnd + 1)
         finish_direct(rnd - 1)
         finish_diagonal(rnd - 1)
+        if rnd < LINE - 1:
+
+            @pl.when(u == 0)
+            def _(peer=others[rnd]):
+                toward(peer, True)
+
         if rnd == LINE - 1:
             for done in range(LINE - 2):
                 drain(done)
                 multiply(done, every, True, True)
+                deliver(done).start()
         relay(rnd)
     last = LINE - 1
     drain(last - 1)
     multiply(last - 1, every, True, True)
+    deliver(last - 1).start()
     finish_direct(last)
     from_core(last, CORE_OWN, sc)
     multiply(last, [s // 2], True, False)
@@ -204,8 +216,17 @@
     finish_diagonal(last)
     from_core(last, CORE_DIAGONAL, twin(sd))
     multiply(last, [sd // 2], False, True)
+    deliver(last).start()
+    for rnd in range(LINE):
+        deliver(rnd).wait()
     for copy in started:
         copy.wait_send()
+    toward(others[0], False)
+    toward(others[2], False)
+
+    @pl.when(u == 0)
+    def _():
+        toward(others[1], False)
 
 
 def in_one_kernel(spectra):
@@ -214,18 +235,20 @@
     return pl.pallas_call(
         functools.partial(kernel, rows, cols, -1.0 / math.sqrt(full)),
         out_shape=jax.ShapeDtypeStruct((1, parts, rows, full), jnp.float32),
-        in_specs=[pl.BlockSpec(memory_space=pl.ANY)],
-        out_specs=pl.BlockSpec(memory_space=pltpu.VMEM),
+        in_specs=[pl.BlockSpec(memory_space=pltpu.HBM)],
+        out_specs=pl.BlockSpec(memory_space=pl.ANY),
         scratch_shapes=[
             pltpu.VMEM((parts, LINE, rows * PLANE, cols), jnp.bfloat16),
+            pltpu.VMEM((parts, rows, full), jnp.float32),
             pltpu.SemaphoreType.DMA,
+            pltpu.SemaphoreType.DMA((LINE,)),
             pltpu.SemaphoreType.DMA((LINE, 2)),
             pltpu.SemaphoreType.DMA((LINE, 2)),
             pltpu.SemaphoreType.DMA((LINE, KINDS)),
             pltpu.SemaphoreType.DMA((LINE, KINDS)),
         ],
         compiler_params=pltpu.CompilerParams(
-            collective_id=0, has_side_effects=True, vmem_limit_bytes=62 * 2**20
+            collective_id=0, has_side_effects=True, vmem_limit_bytes=28 * 2**20
         ),
     )(spectra)
 

time: 107 us -> 82.1 us (0.77)
  Pallas kernels: 102 us -> 78.3 us
  local copies, waits for them, and re-layouts: 4.7 us -> 3.61 us
    pallas_call x1, Pallas kernels: 102 us -> 78.3 us  [in_one_kernel(): pl.pallas_call(functools.partial(kernel, rows, cols, -1.0 / math.sqrt(ful...]
    unnamed x1 -> x3, local copies, waits for them, and re-layouts: 4.7 us -> 3.61 us
where the time goes in v2:
time: 82.1 us; the launch traced here: 81.9 us
  Pallas kernels  78.3 us (95%)
  local copies, waits for them, and re-layouts  3.61 us (4%)
    pallas_call x1, Pallas kernels, in_one_kernel(): pl.pallas_call(functools.partial(kernel, rows, cols, -1.0 / math.sqrt(ful...  78.3 us
    unnamed x3, local copies, waits for them, and re-layouts  3.61 us

profile of v2, /device:TPU:1, one launch (start us, length us, event | category | flops | bytes accessed | tf_op | source)
XLA Modules:
  0.0 81.9 jit_solution(4715474872112620111)
XLA Ops:
  0.0 0.0 copy-start
  0.0 1.6 %copy-done = bf16[4,2,256,512]{3,2,1,0:T(8,128)(2,1)S(1)} copy-done((bf16[4,2,256,512]{3,2,1,0:T(8,128)(2,1)S(1)}, bf16[4,2,256,512]{3,2,1,0:T(8,128)(2,1)}, u32[]{:S(2)}) %copy-start) | copy-done | bytes 2097176
  1.6 78.3 %shard_map.17 = f32[1,2,256,2048]{3,2,1,0:T(8,128)S(1)} custom-call(bf16[4,2,256,512]{3,2,1,0:T(8,128)(2,1)S(1)} %copy-done), custom_call_target="tpu_custom_call" | custom-call | tf_op jit(solution)/shard_map/pallas_call | solution.py:235
  79.9 2.0 %copy.3 = f32[1,2,256,2048]{3,2,1,0:T(8,128)} copy(f32[1,2,256,2048]{3,2,1,0:T(8,128)S(1)} %shard_map.17) | data formatting | bytes 8388608
Async XLA Ops:
  0.0 1.6 %copy-start = (bf16[4,2,256,512]{3,2,1,0:T(8,128)(2,1)S(1)}, bf16[4,2,256,512]{3,2,1,0:T(8,128)(2,1)}, u32[]{:S(2)}) copy-start(bf16[4,2,256,512]{3,2,1,0:T(8,128)(2,1)} %x_ref.1) | copy-start | bytes 6291460

commit v3 on v2

--- a/solution.py
+++ b/solution.py
@@ -89,11 +89,13 @@
             device_id_type=MESH,
         ).wait_recv()
 
-    def send_own(rnd):
-        for part, kind, target in ((0, FROM_X, sx), (1, FROM_Y, sy), (1, FROM_X, sx), (0, FROM_Y, sy)):
+    def send_relayed(rnd):
+        for part, kind, target in ((0, FROM_X, sx), (1, FROM_Y, sy), (0, CORE_OWN, sc), (1, CORE_OWN, sc)):
             push(rnd, kind, part, s, target, x_ref.at[z, part] if rnd == 0 else None)
-        for part in range(2):
-            push(rnd, CORE_OWN, part, s, sc, x_ref.at[z, part] if rnd == 0 else None)
+
+    def send_direct(rnd):
+        for part, kind, target in ((1, FROM_X, sx), (0, FROM_Y, sy)):
+            push(rnd, kind, part, s, target, x_ref.at[z, part] if rnd == 0 else None)
 
     def relay(rnd):
         arrive(rnd, FROM_X, 0, sx)
@@ -156,6 +158,29 @@
             acc[0, :, wide] = real * scale if last else real
             acc[1, :, wide] = imag * scale if last else imag
 
+    def multiply_part(part, chip, last, first=0, deep=cols):
+        column = order[-1]
+
+        @pl.loop(0, cols // tile)
+        def _(t):
+            lanes = pl.ds(pl.multiple_of(t * tile, tile), tile)
+            wide = pl.ds(pl.multiple_of(column * cols + t * tile, tile), tile)
+            if deep == cols:
+                left = [g[p, chip, pl.ds(s * rows, rows), :] for p in range(2)]
+            else:
+                span = pl.ds(pl.multiple_of(first, rows), rows)
+                left = [g[p, chip, pl.ds(s * rows, rows), span] for p in range(2)]
+            right = g[part, column, pl.ds(chip * cols + first, deep), lanes]
+            dot = functools.partial(jnp.dot, preferred_element_type=jnp.float32)
+            a, b = dot(left[part], right), dot(left[1 - part], right)
+            real = acc[0, :, wide] + (a if part == 0 else -a)
+            imag = acc[1, :, wide] + b
+            acc[0, :, wide] = real * scale if last else real
+            acc[1, :, wide] = imag * scale if last else imag
+
+    def multiply_shot(part, shot, last):
+        multiply_part(part, shot // 2, last, (shot % 2) * rows, rows)
+
     def deliver(rnd):
         lanes = pl.ds(pl.multiple_of(order[rnd] * cols, cols), cols)
         return pltpu.make_async_copy(acc.at[:, :, lanes], out_ref.at[0, :, :, lanes], out_sem.at[rnd])
@@ -170,7 +195,8 @@
             copy.start() if begin else copy.wait_send()
 
     toward(others[0], True)
-    send_own(0)
+    send_relayed(0)
+    send_direct(0)
 
     @pl.when(u == 1)
     def _():
@@ -187,9 +213,14 @@
     for rnd in range(1, LINE):
         for part in range(2):
             line_arrival(order[rnd], part).wait_recv()
-        send_own(rnd)
+        send_relayed(rnd)
         finish_direct(rnd - 1)
+        if rnd == LINE - 1:
+            drain(0)
+            multiply(0, every, True, True)
+            deliver(0).start()
         finish_diagonal(rnd - 1)
+        send_direct(rnd)
         if rnd < LINE - 1:
 
             @pl.when(u == 0)
@@ -197,25 +228,31 @@
                 toward(peer, True)
 
         if rnd == LINE - 1:
-            for done in range(LINE - 2):
-                drain(done)
-                multiply(done, every, True, True)
-                deliver(done).start()
+            drain(1)
+            multiply(1, every, True, True)
+            deliver(1).start()
         relay(rnd)
     last = LINE - 1
     drain(last - 1)
     multiply(last - 1, every, True, True)
     deliver(last - 1).start()
-    finish_direct(last)
     from_core(last, CORE_OWN, sc)
     multiply(last, [s // 2], True, False)
-    from_core(last, CORE_X, twin(sx))
-    multiply(last, [sx // 2], False, False)
-    from_core(last, CORE_Y, twin(sy))
-    multiply(last, [sy // 2], False, False)
+    finish_direct(last)
+    arrive(last, CORE_X, 0, twin(sx))
+    multiply_part(0, sx // 2, False)
+    arrive(last, CORE_Y, 1, twin(sy))
+    multiply_part(1, sy // 2, False)
+    arrive(last, CORE_X, 1, twin(sx))
+    multiply_part(1, sx // 2, False)
+    arrive(last, CORE_Y, 0, twin(sy))
+    multiply_part(0, sy // 2, False)
     finish_diagonal(last)
-    from_core(last, CORE_DIAGONAL, twin(sd))
-    multiply(last, [sd // 2], False, True)
+    for part in range(2):
+        multiply_shot(part, sd, False)
+    for part in range(2):
+        arrive(last, CORE_DIAGONAL, part, twin(sd))
+        multiply_shot(part, twin(sd), part == 1)
     deliver(last).start()
     for rnd in range(LINE):
         deliver(rnd).wait()
@@ -250,7 +287,7 @@
         compiler_params=pltpu.CompilerParams(
             collective_id=0, has_side_effects=True, vmem_limit_bytes=28 * 2**20
         ),
-    )(spectra)
+    )(pltpu.with_memory_space_constraint(spectra, pltpu.HBM))
 
 
 def by_collectives(spectra):

time: 82.1 us -> 80.4 us (0.979)
  local copies, waits for them, and re-layouts: 3.61 us -> 2.02 us
    unnamed x3 -> x1, local copies, waits for them, and re-layouts: 3.61 us -> 2.02 us
where the time goes in v3:
time: 80.4 us; the launch traced here: 80.2 us
  Pallas kernels  78.2 us (97%)
  local copies, waits for them, and re-layouts  2.02 us (3%)
    pallas_call x1, Pallas kernels, in_one_kernel(): pl.pallas_call(functools.partial(kernel, rows, cols, -1.0 / math.sqrt(ful...  78.2 us
    unnamed x1, local copies, waits for them, and re-layouts  2.02 us

profile of v3, /device:TPU:1, one launch (start us, length us, event | category | flops | bytes accessed | tf_op | source)
XLA Modules:
  0.0 80.2 jit_solution(4437995485837158445)
XLA Ops:
  0.0 78.2 %shard_map.17 = f32[1,2,256,2048]{3,2,1,0:T(8,128)S(1)} custom-call(bf16[4,2,256,512]{3,2,1,0:T(8,128)(2,1)} %x_ref.1), custom_call_target="tpu_custom_call" | custom-call | tf_op jit(solution)/shard_map/pallas_call | solution.py:272
  78.2 2.0 %copy.3 = f32[1,2,256,2048]{3,2,1,0:T(8,128)} copy(f32[1,2,256,2048]{3,2,1,0:T(8,128)S(1)} %shard_map.17) | data formatting | bytes 8388608

commit v4 on v3

--- a/solution.py
+++ b/solution.py
@@ -129,7 +129,7 @@
         from_core(rnd, CORE_Y, twin(sy))
         from_core(rnd, CORE_DIAGONAL, twin(sd))
 
-    tile = 256
+    tile = 512
 
     def chip_product(column, chip, lanes):
         left = [g[part, chip, pl.ds(s * rows, rows), :] for part in range(2)]
@@ -219,8 +219,11 @@
             drain(0)
             multiply(0, every, True, True)
             deliver(0).start()
+        if rnd == LINE - 1:
+            send_direct(rnd)
         finish_diagonal(rnd - 1)
-        send_direct(rnd)
+        if rnd < LINE - 1:
+            send_direct(rnd)
         if rnd < LINE - 1:
 
             @pl.when(u == 0)

time: 80.4 us -> 80.1 us (level)
  no operation moved by 1% of the time
where the time goes in v4:
time: 80.1 us; the launch traced here: 80 us
  Pallas kernels  77.9 us (97%)
  local copies, waits for them, and re-layouts  2.02 us (3%)
    pallas_call x1, Pallas kernels, in_one_kernel(): pl.pallas_call(functools.partial(kernel, rows, cols, -1.0 / math.sqrt(ful...  77.9 us
    unnamed x1, local copies, waits for them, and re-layouts  2.02 us

profile of v4, /device:TPU:1, one launch (start us, length us, event | category | flops | bytes accessed | tf_op | source)
XLA Modules:
  0.0 80.0 jit_solution(17855350963117508677)
XLA Ops:
  0.0 77.9 %shard_map.17 = f32[1,2,256,2048]{3,2,1,0:T(8,128)S(1)} custom-call(bf16[4,2,256,512]{3,2,1,0:T(8,128)(2,1)} %x_ref.1), custom_call_target="tpu_custom_call" | custom-call | tf_op jit(solution)/shard_map/pallas_call | solution.py:275
  77.9 2.0 %copy.3 = f32[1,2,256,2048]{3,2,1,0:T(8,128)} copy(f32[1,2,256,2048]{3,2,1,0:T(8,128)S(1)} %shard_map.17) | data formatting | bytes 8388608

commit v5 on v3

--- a/solution.py
+++ b/solution.py
@@ -129,7 +129,7 @@
         from_core(rnd, CORE_Y, twin(sy))
         from_core(rnd, CORE_DIAGONAL, twin(sd))
 
-    tile = 256
+    tile = 512
 
     def chip_product(column, chip, lanes):
         left = [g[part, chip, pl.ds(s * rows, rows), :] for part in range(2)]

time: 80.4 us -> 80.1 us (level)
  no operation moved by 1% of the time
where the time goes in v5:
time: 80.1 us; the launch traced here: 80 us
  Pallas kernels  77.9 us (97%)
  local copies, waits for them, and re-layouts  2.02 us (3%)
    pallas_call x1, Pallas kernels, in_one_kernel(): pl.pallas_call(functools.partial(kernel, rows, cols, -1.0 / math.sqrt(ful...  77.9 us
    unnamed x1, local copies, waits for them, and re-layouts  2.02 us

profile of v5, /device:TPU:1, one launch (start us, length us, event | category | flops | bytes accessed | tf_op | source)
XLA Modules:
  0.0 80.0 jit_solution(15096741423687976559)
XLA Ops:
  0.0 77.9 %shard_map.17 = f32[1,2,256,2048]{3,2,1,0:T(8,128)S(1)} custom-call(bf16[4,2,256,512]{3,2,1,0:T(8,128)(2,1)} %x_ref.1), custom_call_target="tpu_custom_call" | custom-call | tf_op jit(solution)/shard_map/pallas_call | solution.py:272
  77.9 2.0 %copy.3 = f32[1,2,256,2048]{3,2,1,0:T(8,128)} copy(f32[1,2,256,2048]{3,2,1,0:T(8,128)S(1)} %shard_map.17) | data formatting | bytes 8388608

commit v6 on v5

--- a/solution.py
+++ b/solution.py
@@ -188,14 +188,15 @@
     every = range(LINE)
 
     own = pltpu.make_async_copy(x_ref.at[z], g.at[:, z, pl.ds(s * rows, rows), :], own_sem)
-    own.start()
+
     def toward(peer, begin):
         for part in range(2):
             copy = along_line(peer, part)
             copy.start() if begin else copy.wait_send()
 
+    send_relayed(0)
     toward(others[0], True)
-    send_relayed(0)
+    own.start()
     send_direct(0)
 
     @pl.when(u == 1)

time: 80.1 us -> 80.1 us (level)
  no operation moved by 1% of the time
where the time goes in v6:
time: 80.1 us; the launch traced here: 79.9 us
  Pallas kernels  77.9 us (97%)
  local copies, waits for them, and re-layouts  2.02 us (3%)
    pallas_call x1, Pallas kernels, in_one_kernel(): pl.pallas_call(functools.partial(kernel, rows, cols, -1.0 / math.sqrt(ful...  77.9 us
    unnamed x1, local copies, waits for them, and re-layouts  2.02 us

profile of v6, /device:TPU:1, one launch (start us, length us, event | category | flops | bytes accessed | tf_op | source)
XLA Modules:
  0.0 79.9 jit_solution(1947490578149848442)
XLA Ops:
  0.0 77.9 %shard_map.17 = f32[1,2,256,2048]{3,2,1,0:T(8,128)S(1)} custom-call(bf16[4,2,256,512]{3,2,1,0:T(8,128)(2,1)} %x_ref.1), custom_call_target="tpu_custom_call" | custom-call | tf_op jit(solution)/shard_map/pallas_call | solution.py:273
  77.9 2.0 %copy.3 = f32[1,2,256,2048]{3,2,1,0:T(8,128)} copy(f32[1,2,256,2048]{3,2,1,0:T(8,128)S(1)} %shard_map.17) | data formatting | bytes 8388608
